TPU v7x, 256 devices: a whole 4x4x8 slice. The times are simulated.
256 devices in a mesh: dp: 32 (over x, y, core), ctx: 8 (over z).
Axes of the slice: x: 4, y: 4, z: 8, core: 2. Of those that a mesh axis runs over, the one named last changes fastest.
Arguments:
- cotangent: bfloat16 [32, 4096, 8192], P('dp', 'ctx'), may hold values from -6 to 6
- out_weight: bfloat16 [256, 8192], P(None, 'ctx'), may hold values from -0.0625 to 0.0625
- head_input: bfloat16 [32, 4096, 256], P('dp', 'ctx'), may hold values from -6 to 6
- injector: bfloat16 [32, 4096, 128], P('dp', 'ctx'), may hold values from -0.59765625 to 0.59765625
- readout: bfloat16 [32, 4096, 128], P('dp', 'ctx'), may hold values from -0.59765625 to 0.59765625
- decay_code: int32 [32, 4096, 2], P('dp', 'ctx'), may hold values from 1 to 40960
- decay_rate: float32 [2], replicated, may hold values from 4.8828125e-06 to 0.0061035156
- start_state: float32 [32, 8, 2, 128, 128], P('dp', 'ctx'), may hold values from -6 to 6
Outputs:
- gradient_input: bfloat16 [32, 4096, 256], P('dp', 'ctx')
- gradient_injector: float32 [32, 4096, 128], P('dp', 'ctx')
- gradient_readout: float32 [32, 4096, 128], P('dp', 'ctx')
- gradient_weight: float32 [256, 8192], P('ctx', 'dp')
- gradient_rate: float32 [2], replicated
All inputs are finite; a program needn't handle non-finite values.
Results may differ from a plain program's by a relative error of at most 0.0049.
Values may be sent and summed in bfloat16 or wider, within the bound.
No kernel may reach another device: no remote copies, remote signals or barrier semaphores. Data moves between devices by JAX's collectives and lax.ppermute only.
A program may use at most 128 MiB of HBM per device.

v0:
```python
import jax
import jax.numpy as jnp
from jax import lax
from jax.sharding import PartitionSpec as P

precise = lax.Precision.HIGHEST


def carried_in(value, axis, join, neutral):
    count, mine = (lax.axis_size(axis), lax.axis_index(axis))
    pieces = jax.tree.map(lambda part: lax.all_gather(part, axis), value)
    pieces = jax.tree.map(lambda part: part[::-1], pieces)
    mine = count - 1 - mine
    total = jax.tree.map(
        lambda part, zero: jnp.full_like(part, 0) + jnp.asarray(zero, part.dtype), value, neutral
    )

    def lap(position, total):
        longer = join(total, jax.tree.map(lambda part: part[position], pieces))
        return jax.tree.map(lambda new, old: jnp.where(position < mine, new, old), longer, total)

    return lax.fori_loop(0, count - 1, lap, total)


def decay_table(log_decay):
    cumulative = jnp.cumsum(log_decay, axis=0)
    length = log_decay.shape[0]
    row_index = lax.broadcasted_iota(jnp.int32, (length, length), 0)
    col_index = lax.broadcasted_iota(jnp.int32, (length, length), 1)
    causal = (row_index >= col_index)[None]
    spread = cumulative.T[:, :, None] - cumulative.T[:, None, :]
    weights = jnp.where(causal, jnp.exp(jnp.where(causal, spread, 0.0)), 0.0)
    return (cumulative, weights)


def forward_shard(head_input, injector, readout, log_decay, start_state):
    length, heads_count = log_decay.shape
    cumulative, weights = decay_table(log_decay)
    intersection = jnp.dot(readout, injector.T, preferred_element_type=jnp.float32)
    mixing = intersection[None] * weights
    inputs_heads = head_input.reshape(length, heads_count, -1).astype(jnp.float32)
    within = jnp.einsum("hts,shp->thp", mixing, inputs_heads, precision=precise)
    carried = jnp.einsum("tn,hpn->thp", readout.astype(jnp.float32), start_state, precision=precise)
    outputs = within + jnp.exp(cumulative)[:, :, None] * carried
    return outputs.reshape(length, -1).astype(jnp.bfloat16)


def chain_piece(readout, output_grad, log_decay):
    length, heads_count = log_decay.shape
    cumulative = jnp.cumsum(log_decay, axis=0)
    grad_heads = output_grad.reshape(length, heads_count, -1).astype(jnp.float32)
    scaled = jnp.exp(cumulative)[:, :, None] * readout.astype(jnp.float32)[:, None, :]
    adjoint = jnp.einsum("thp,thn->hpn", grad_heads, scaled, precision=precise)
    return (jnp.exp(cumulative[-1]), adjoint)


def backward_shard(head_input, injector, readout, output_grad, log_decay, start_state, incoming):
    length, heads_count = log_decay.shape
    cumulative, weights = decay_table(log_decay)
    inputs_narrow = head_input.reshape(length, heads_count, -1)
    grad_narrow = output_grad.reshape(length, heads_count, -1)
    inputs_heads = inputs_narrow.astype(jnp.float32)
    grad_heads = grad_narrow.astype(jnp.float32)
    inject_float = injector.astype(jnp.float32)
    read_float = readout.astype(jnp.float32)
    intersection = jnp.dot(readout, injector.T, preferred_element_type=jnp.float32)
    mixing = intersection[None] * weights
    to_end = jnp.exp(cumulative[-1][None, :] - cumulative)
    from_start = jnp.exp(cumulative)
    entering = jnp.einsum("sn,hpn->shp", inject_float, incoming, precision=precise)
    grad_input = (
        jnp.einsum("hts,thp->shp", mixing, grad_heads, precision=precise)
        + to_end[:, :, None] * entering
    )
    pairing = (
        jnp.einsum("thp,shp->hts", grad_narrow, inputs_narrow, preferred_element_type=jnp.float32)
        * weights
    )
    through_start = jnp.einsum("thp,hpn->thn", grad_heads, start_state, precision=precise)
    grad_read = jnp.einsum("hts,sn->tn", pairing, inject_float, precision=precise)
    grad_read = grad_read + jnp.einsum("th,thn->tn", from_start, through_start, precision=precise)
    input_state = jnp.einsum("shp,hpn->shn", inputs_heads, incoming, precision=precise)
    grad_inject = jnp.einsum("hts,tn->sn", pairing, read_float, precision=precise)
    grad_inject = grad_inject + jnp.einsum("sh,shn->sn", to_end, input_state, precision=precise)
    products = intersection[None] * pairing
    carried = (
        jnp.einsum("tn,hpn->thp", read_float, start_state, precision=precise)
        * from_start[:, :, None]
    )
    reaching = to_end * jnp.einsum("shn,sn->sh", input_state, inject_float, precision=precise)
    end_term = from_start[-1] * jnp.einsum(
        "hpn,hpn->h", incoming, start_state, precision=precise
    ) + jnp.sum(reaching, axis=0)
    cumul_grad = jnp.sum(products, axis=2).T - jnp.sum(products, axis=1).T
    cumul_grad = cumul_grad + jnp.sum(grad_heads * carried, axis=2) - reaching
    is_last = lax.broadcasted_iota(jnp.int32, (length, 1), 0) == length - 1
    cumul_grad = cumul_grad + jnp.where(is_last, end_term[None, :], 0.0)
    decay_grad = jnp.flip(jnp.cumsum(jnp.flip(cumul_grad, 0), axis=0), 0)
    rate_terms = jnp.sum(decay_grad * log_decay, axis=0)
    return (grad_input.reshape(length, -1).astype(jnp.bfloat16), grad_inject, grad_read, rate_terms)


def combine(earlier, later):
    return (later[0] * earlier[0], later[1] + later[0][:, None, None] * earlier[1])


def local(
    cotangent, out_weight, head_input, injector, readout, decay_code, decay_rate, start_state
):
    grad_out = cotangent[0]
    inputs_local = head_input[0]
    inject_local = injector[0]
    read_local = readout[0]
    state_local = start_state[0, 0]
    length = grad_out.shape[0]
    output_grad = lax.dot_general(
        grad_out,
        lax.all_gather(out_weight, "ctx", axis=1, tiled=True),
        (((1,), (1,)), ((), ())),
        preferred_element_type=jnp.float32,
    ).astype(jnp.bfloat16)
    log_decay = -decay_rate[None, :] * decay_code[0].astype(jnp.float32)
    decay_total, adjoint = chain_piece(read_local, output_grad, log_decay)
    identity = (jnp.ones_like(decay_total), jnp.zeros_like(adjoint))
    incoming = carried_in((decay_total, adjoint), "ctx", combine, identity)[1]
    outputs = forward_shard(inputs_local, inject_local, read_local, log_decay, state_local)
    local_weight = lax.dot_general(
        outputs, grad_out, (((0,), (0,)), ((), ())), preferred_element_type=jnp.float32
    )
    data_part = lax.psum_scatter(local_weight, "dp", scatter_dimension=1, tiled=True)
    weight_part = lax.psum_scatter(data_part, "ctx", scatter_dimension=0, tiled=True)
    grad_input, grad_inject, grad_read, rate_terms = backward_shard(
        inputs_local, inject_local, read_local, output_grad, log_decay, state_local, incoming
    )
    tokens_all = length * lax.axis_size("dp") * lax.axis_size("ctx")
    rate_sum = lax.psum(rate_terms, ("dp", "ctx"))
    return (
        grad_input[None],
        grad_inject[None],
        grad_read[None],
        weight_part,
        rate_sum / tokens_all,
    )


def solution(mesh):
    in_specs = (
        P("dp", "ctx", None),
        P(None, "ctx"),
        P("dp", "ctx", None),
        P("dp", "ctx", None),
        P("dp", "ctx", None),
        P("dp", "ctx", None),
        P(),
        P("dp", "ctx", None, None, None),
    )
    out_specs = (
        P("dp", "ctx", None),
        P("dp", "ctx", None),
        P("dp", "ctx", None),
        P("ctx", "dp"),
        P(),
    )
    return jax.shard_map(local, mesh=mesh, in_specs=in_specs, out_specs=out_specs, check_vma=False)
```

profile of v0, /device:TPU:2, one launch (start us, length us, event | category | flops | bytes accessed | tf_op | source)
XLA Modules:
  0.0 262.4 jit_solution(3269358175071123547)
XLA Ops:
  7.2 0.7 all-gather.5.cloned.1.call-update
  7.9 0.7 neg.4
  8.6 0.8 fusion.61
  9.4 0.6 reduce-window.14
  10.3 0.9 bitcast_convert_fusion.1
  11.5 56.1 %all-gather.5.cloned.1.call-done = bf16[256,8192]{1,0:T(8,128)(2,1)} async-done(((bf16[256,1024]{1,0:T(8,128)(2,1)}), bf16[256,8192]{1,0:T(8,128)(2,1)}) %all-gather.5.cloned.1.call-update) | async-done | bytes 4194320 | tf_op jit(solution)/shard_map/all_gather | solution.py:118
  67.6 6.9 %fusion.26 = bf16[512,256]{0,1:T(8,128)(2,1)S(1)} fusion(bf16[256,8192]{1,0:T(8,128)(2,1)} %all-gather.5.cloned.1.call-done, bf16[1,512,8192]{2,1,0:T(8,128)(2,1)} %param.10), kind=kOutput, calls=%fused_computation.24 | convolution fusion | flops 2147614720 | bytes 12845056 | tf_op jit(solution)/shard_map/dot_general | solution.py:116
  74.6 1.1 fusion.43
  76.8 2.0 fusion.22
  78.7 9.1 %fusion.1 = f32[256,8192]{1,0:T(8,128)} fusion(bf16[512,256]{0,1:T(8,128)(2,1)S(1)} %bitcast.164, bf16[1,512,8192]{2,1,0:T(8,128)(2,1)} %param.10), kind=kOutput, calls=%fused_computation.3 | convolution fusion | flops 2147483648 | bytes 17039360 | tf_op jit(solution)/shard_map/dot_general | solution.py:127
  88.0 14.7 %all-gather.1 = f32[8,1,2]{2,1,0:T(1,128)S(1)} all-gather(f32[1,1,2]{2,1,0:T(1,128)S(1)} %bitcast.175), channel_id=1, replica_groups=mesh['dp'=32,'ctx'=8] {'ctx'}, dimensions={0}, use_global_device_ids=true | all-gather | bytes 72 | tf_op jit(solution)/shard_map/all_gather | solution.py:11
  104.0 4.4 %fusion.45 = f32[512,1,128]{2,1,0:T(1,128)} fusion(f32[512,2,1]{1,2,0:T(1,128)S(1)} %copy.72, f32[512,2,128]{2,0,1:T(8,128)S(1)} %convolution_bitcast_fusion), kind=kOutput, calls=%fused_computation.47 | convolution fusion | flops 1572864 | bytes 790528 | tf_op jit(solution)/shard_map/th,thn->tn/dot_general | solution.py:81
  108.4 2.4 fusion.11
  110.8 2.2 multiply_reduce_fusion
  113.1 1.3 rev.13
  114.5 0.9 while.14
  116.6 0.6 reduce-window.16
  118.2 1.3 fusion.29
  119.5 75.2 %psum.7 = f32[2]{0:T(128)S(1)} all-reduce(f32[2]{0:T(128)S(1)} %multiply_reduce_fusion.3), channel_id=1, replica_groups=mesh['dp'=32,'ctx'=8] {'dp','ctx'}, use_global_device_ids=true, to_apply=%region_14.15 | all-reduce | flops 2 | bytes 16 | tf_op jit(solution)/shard_map/psum | solution.py:136
  194.9 21.4 %reduce-scatter.3.cloned.1.call-done = f32[256,256]{1,0:T(8,128)} async-done(((f32[256,8192]{1,0:T(8,128)}), f32[256,256]{1,0:T(8,128)}) %reduce-scatter.3.cloned.1.call-update) | async-done | bytes 262160 | tf_op jit(solution)/shard_map/reduce_scatter | solution.py:130
  216.7 0.8 copy.62
  217.6 1.7 fusion.30
  219.3 0.5 broadcast_multiply_fusion
  219.8 36.1 %reduce-scatter.5.cloned.1.call-done = f32[32,256]{1,0:T(8,128)} async-done(((f32[256,256]{1,0:T(8,128)}), f32[32,256]{1,0:T(8,128)}) %reduce-scatter.5.cloned.1.call-update) | async-done | bytes 32784 | tf_op jit(solution)/shard_map/reduce_scatter | solution.py:131
  (76 shorter events, 6.6 us)
Async XLA Ops:
  7.2 60.4 %all-gather.5.cloned.1.call-start = ((), (), s32[]{:S(2)}) async-start(), calls=%async_computation.2 | async-start | bytes 4718592 | tf_op jit(solution)/shard_map/all_gather | solution.py:118
  7.9 105.2 %all-gather.7.cloned.1.call-start = ((), (), s32[]{:S(2)}) async-start(), calls=%async_computation.5 | async-start | bytes 1179648 | tf_op jit(solution)/shard_map/all_gather | solution.py:11
  11.5 64.2 %copy-start.4 = (bf16[1,512,256]{2,1,0:T(8,128)(2,1)S(1)}, bf16[1,512,256]{2,1,0:T(8,128)(2,1)}, u32[]{:S(2)}) copy-start(bf16[1,512,256]{2,1,0:T(8,128)(2,1)} %param.12) | copy-start | bytes 786436
  11.5 64.5 %copy-start = (bf16[1,512,128]{2,1,0:T(8,128)(2,1)S(1)}, bf16[1,512,128]{2,1,0:T(8,128)(2,1)}, u32[]{:S(2)}) copy-start(bf16[1,512,128]{2,1,0:T(8,128)(2,1)} %param.13) | copy-start | bytes 393220
  11.5 64.5 %copy-start.1 = (bf16[1,512,128]{2,1,0:T(8,128)(2,1)S(1)}, bf16[1,512,128]{2,1,0:T(8,128)(2,1)}, u32[]{:S(2)}) copy-start(bf16[1,512,128]{2,1,0:T(8,128)(2,1)} %param.14) | copy-start | bytes 393220
  74.5 1.8 copy-start.2
  75.7 140.6 %reduce-scatter.3.cloned.1.call-start = ((), (), s32[]{:S(2)}) async-start(), calls=%async_computation.3 | async-start | bytes 8650752 | tf_op jit(solution)/shard_map/reduce_scatter | solution.py:130
  76.0 32.4 %copy-start.5 = (pred[512,512]{1,0:T(8,128)(4,1)}, pred[512,512]{1,0:T(8,128)(4,1)S(1)}, u32[]{:S(2)}) copy-start(pred[512,512]{1,0:T(8,128)(4,1)S(1)} %iota_compare_fusion) | copy-start | bytes 786436
  87.8 168.0 %reduce-scatter.5.cloned.1.call-start = ((), (), s32[]{:S(2)}) async-start(), calls=%async_computation.4 | async-start | bytes 294912 | tf_op jit(solution)/shard_map/reduce_scatter | solution.py:131
  114.4 3.5 %copy-start.7 = (s32[1,512,2]{1,2,0:T(2,128)S(1)}, s32[1,512,2]{1,2,0:T(2,128)}, u32[]{:S(2)}) copy-start(s32[1,512,2]{1,2,0:T(2,128)} %param.15) | copy-start | bytes 12292
  114.5 3.7 %copy-start.6 = (f32[512,1,128]{2,1,0:T(1,128)S(1)}, f32[512,1,128]{2,1,0:T(1,128)}, u32[]{:S(2)}) copy-start(f32[512,1,128]{2,1,0:T(1,128)} %fusion.45) | copy-start | bytes 786436
  115.5 100.8 %copy-start.3 = (f32[512,2,128]{0,2,1:T(8,128)S(1)}, f32[512,2,128]{0,2,1:T(8,128)}, u32[]{:S(2)}) copy-start(f32[512,2,128]{0,2,1:T(8,128)} %fusion.11) | copy-start | bytes 1572868
Sparse Core Ops, SparseCore 0:
  9.8 57.7 all-gather.4
  75.8 37.3 all-gather.6
  117.2 99.0 reduce-scatter.2
  219.4 36.4 reduce-scatter.4
where the time goes:
time: 263 us; the launch traced here: 262 us
  waiting for transfers between devices  114 us (43%)
  blocking collectives  89.9 us (34%)
  matrix products  33.1 us (13%)
  between operations  14 us (5%)
  other arithmetic  5.93 us (2%)
  local copies, waits for them, and re-layouts  4.61 us (2%)
    psum x1, blocking collectives, local(): rate_sum = lax.psum(rate_terms, ('dp', 'ctx'))  75.2 us
    all_gather x1, waiting for transfers between devices, local(): lax.all_gather(out_weight, 'ctx', axis=1, tiled=True)  56.1 us
    reduce_scatter x1, waiting for transfers between devices, local(): lax.psum_scatter(data_part, 'ctx', scatter_dimension=0, tiled=True)  36.1 us
    reduce_scatter x1, waiting for transfers between devices, local(): lax.psum_scatter(local_weight, 'dp', scatter_dimension=1, tiled=True)  21.4 us
    all_gather x1, blocking collectives, carried_in(): pieces = jax.tree.map(lambda part: lax.all_gather(part, axis), value)  14.7 us
    dot_general x1, matrix products, local(): lax.dot_general(outputs, grad_out, (((0,), (0,)), ((), ())), preferred_el...  9.06 us
    dot_general x1, matrix products, local(): lax.dot_general(grad_out, lax.all_gather(out_weight, 'ctx', axis=1, tiled...  6.93 us
  transfers between devices with their start and end apart: 4, of which 4 were waited for; matrix products, arithmetic and copies ran while one was open for 14% of the time, Pallas kernels for 0%

commit v1 on v0

--- a/solution.py
+++ b/solution.py
@@ -4,6 +4,11 @@
 from jax.sharding import PartitionSpec as P
 
 precise = lax.Precision.HIGHEST
+
+
+def tiled_gather(array, axis, dim):
+    copies = jnp.concatenate([array] * lax.axis_size(axis), axis=dim)
+    return lax.all_to_all(copies, axis, dim, dim, tiled=True)
 
 
 def carried_in(value, axis, join, neutral):
@@ -115,7 +120,7 @@
     length = grad_out.shape[0]
     output_grad = lax.dot_general(
         grad_out,
-        lax.all_gather(out_weight, "ctx", axis=1, tiled=True),
+        tiled_gather(out_weight, "ctx", 1),
         (((1,), (1,)), ((), ())),
         preferred_element_type=jnp.float32,
     ).astype(jnp.bfloat16)

time: 263 us -> 296 us (1.13)
  local copies, waits for them, and re-layouts: 4.61 us -> 21 us
  waiting for transfers between devices: 114 us -> 123 us
  starting transfers between devices: 0.16 us -> 8.73 us
    all_to_all x0 -> x1, waiting for transfers between devices: none -> 95 us  [tiled_gather(): return lax.all_to_all(copies, axis, dim, dim, tiled=True)]
    all_gather x1 -> x0, waiting for transfers between devices: 56.1 us -> none  [local(): lax.all_gather(out_weight, 'ctx', axis=1, tiled=True)]
    reduce_scatter x1, waiting for transfers between devices: 21.4 us -> 0.03 us  [local(): lax.psum_scatter(local_weight, 'dp', scatter_dimension=1, tiled=True)]
    all_to_all x0 -> x2, local copies, waits for them, and re-layouts: none -> 12.9 us  [tiled_gather(): return lax.all_to_all(copies, axis, dim, dim, tiled=True)]
    all_to_all x0 -> x1, starting transfers between devices: none -> 8.6 us  [tiled_gather(): return lax.all_to_all(copies, axis, dim, dim, tiled=True)]
    reduce_scatter x1, waiting for transfers between devices: 36.1 us -> 28.4 us  [local(): lax.psum_scatter(data_part, 'ctx', scatter_dimension=0, tiled=True)]
    unnamed x21 -> x31, local copies, waits for them, and re-layouts: 1.11 us -> 4.51 us
  transfers between devices with their start and end apart: 4 -> 4, of which waited for: 4 -> 2; matrix products, arithmetic and copies ran while one was open for 14% -> 12% of each run, Pallas kernels for 0% -> 0%
where the time goes in v1:
time: 296 us; the launch traced here: 295 us
  waiting for transfers between devices  123 us (42%)
  blocking collectives  88 us (30%)
  matrix products  34.5 us (12%)
  local copies, waits for them, and re-layouts  21 us (7%)
  between operations  15.8 us (5%)
  starting transfers between devices  8.73 us (3%)
  other arithmetic  3.66 us (1%)
    all_to_all x1, waiting for transfers between devices, tiled_gather(): return lax.all_to_all(copies, axis, dim, dim, tiled=True)  95 us
    psum x1, blocking collectives, local(): rate_sum = lax.psum(rate_terms, ('dp', 'ctx'))  74.2 us
    reduce_scatter x1, waiting for transfers between devices, local(): lax.psum_scatter(data_part, 'ctx', scatter_dimension=0, tiled=True)  28.4 us
    all_gather x1, blocking collectives, carried_in(): pieces = jax.tree.map(lambda part: lax.all_gather(part, axis), value)  13.8 us
    all_to_all x2, local copies, waits for them, and re-layouts, tiled_gather(): return lax.all_to_all(copies, axis, dim, dim, tiled=True)  12.9 us
    dot_general x1, matrix products, local(): lax.dot_general(outputs, grad_out, (((0,), (0,)), ((), ())), preferred_el...  8.95 us
    all_to_all x1, starting transfers between devices, tiled_gather(): return lax.all_to_all(copies, axis, dim, dim, tiled=True)  8.6 us
    dot_general x1, matrix products, local(): lax.dot_general(grad_out, tiled_gather(out_weight, 'ctx', 1), (((1,), (1,...  7.08 us
  transfers between devices with their start and end apart: 4, of which 2 were waited for; matrix products, arithmetic and copies ran while one was open for 12% of the time, Pallas kernels for 0%

profile of v1, /device:TPU:2, one launch (start us, length us, event | category | flops | bytes accessed | tf_op | source)
XLA Modules:
  0.0 295.5 jit_solution(9387877463644981656)
XLA Ops:
  8.0 1.2 copy.52
  9.6 1.9 copy-done
  11.5 6.5 %copy.60 = bf16[256,8,1024]{2,0,1:T(8,128)(2,1)} copy(bf16[256,8,1024]{0,2,1:T(8,128)(2,1)} %bitcast.159) | data formatting | bytes 8388608 | tf_op jit(solution)/shard_map/all_to_all | solution.py:11
  18.0 8.6 %all-to-all-start = ((bf16[256,8,1024]{2,0,1:T(8,128)(2,1)}), bf16[256,8,1024]{2,0,1:T(8,128)(2,1)}, u32[]{:S(2)}, u32[]{:S(2)}) async-start(bf16[256,8,1024]{2,0,1:T(8,128)(2,1)} %copy.60), calls=%async_computation | async-start | bytes 8388608 | tf_op jit(solution)/shard_map/all_to_all | solution.py:11
  26.8 0.6 reduce-window.14
  27.9 95.0 %all-to-all-done = bf16[256,8,1024]{2,0,1:T(8,128)(2,1)} async-done(((bf16[256,8,1024]{2,0,1:T(8,128)(2,1)}), bf16[256,8,1024]{2,0,1:T(8,128)(2,1)}, u32[]{:S(2)}, u32[]{:S(2)}) %all-to-all-start) | async-done | bytes 4194336 | tf_op jit(solution)/shard_map/all_to_all | solution.py:11
  123.0 6.4 %copy.61 = bf16[256,8,1024]{0,2,1:T(8,128)(2,1)} copy(bf16[256,8,1024]{2,0,1:T(8,128)(2,1)} %all-to-all-done) | data formatting | bytes 8388608 | tf_op jit(solution)/shard_map/all_to_all | solution.py:11
  129.4 7.1 %fusion.26 = bf16[256,512]{1,0:T(8,128)(2,1)S(1)} fusion(bf16[256,8192]{0,1:T(8,128)(2,1)} %bitcast.160, bf16[1,512,8192]{2,1,0:T(8,128)(2,1)} %param.10), kind=kOutput, calls=%fused_computation.24 | convolution fusion | flops 2147614720 | bytes 12845056 | tf_op jit(solution)/shard_map/dot_general | solution.py:121
  136.5 1.1 fusion.43
  138.7 2.0 fusion.22
  140.7 9.0 %fusion.1 = f32[256,8192]{1,0:T(8,128)} fusion(bf16[512,256]{0,1:T(8,128)(2,1)S(1)} %bitcast.170, bf16[1,512,8192]{2,1,0:T(8,128)(2,1)} %param.10), kind=kOutput, calls=%fused_computation.3 | convolution fusion | flops 2147483648 | bytes 17039360 | tf_op jit(solution)/shard_map/dot_general | solution.py:132
  149.9 13.8 %all-gather.1 = f32[8,1,2]{2,1,0:T(1,128)S(1)} all-gather(f32[1,1,2]{2,1,0:T(1,128)S(1)} %bitcast.181), channel_id=1, replica_groups=mesh['dp'=32,'ctx'=8] {'ctx'}, dimensions={0}, use_global_device_ids=true | all-gather | bytes 72 | tf_op jit(solution)/shard_map/all_gather | solution.py:16
  164.9 4.4 %fusion.45 = f32[512,1,128]{2,1,0:T(1,128)} fusion(f32[512,2,1]{1,2,0:T(1,128)S(1)} %copy.82, f32[512,2,128]{2,0,1:T(8,128)S(1)} %convolution_bitcast_fusion), kind=kOutput, calls=%fused_computation.47 | convolution fusion | flops 1572864 | bytes 790528 | tf_op jit(solution)/shard_map/th,thn->tn/dot_general | solution.py:86
  169.3 2.4 fusion.11
  171.7 2.5 multiply_reduce_fusion
  174.3 1.4 rev.13
  175.7 0.9 while.14
  177.8 0.6 reduce-window.16
  179.4 1.3 fusion.29
  180.7 74.2 %psum.7 = f32[2]{0:T(128)S(1)} all-reduce(f32[2]{0:T(128)S(1)} %multiply_reduce_fusion.3), channel_id=1, replica_groups=mesh['dp'=32,'ctx'=8] {'dp','ctx'}, use_global_device_ids=true, to_apply=%region_14.15 | all-reduce | flops 2 | bytes 16 | tf_op jit(solution)/shard_map/psum | solution.py:141
  255.2 1.4 fusion.25
  256.6 0.8 copy.72
  257.5 1.7 fusion.30
  259.7 28.4 %reduce-scatter.5.cloned.1.call-done = f32[32,256]{1,0:T(8,128)} async-done(((f32[256,256]{1,0:T(8,128)}), f32[32,256]{1,0:T(8,128)}) %reduce-scatter.5.cloned.1.call-update) | async-done | bytes 32784 | tf_op jit(solution)/shard_map/reduce_scatter | solution.py:136
  (88 shorter events, 7.0 us)
Async XLA Ops:
  9.6 1.9 copy-start
  18.0 8.7 %copy-start.8 = (f32[2]{0:T(128)S(1)}, f32[2]{0:T(128)}, u32[]{:S(2)}) copy-start(f32[2]{0:T(128)} %param.16) | copy-start | bytes 28
  18.0 8.7 %copy-start.7 = (s32[1,512,2]{1,2,0:T(2,128)S(1)}, s32[1,512,2]{1,2,0:T(2,128)}, u32[]{:S(2)}) copy-start(s32[1,512,2]{1,2,0:T(2,128)} %param.15) | copy-start | bytes 12292
  18.0 9.7 %copy-start.2 = (bf16[1,512,128]{2,1,0:T(8,128)(2,1)S(1)}, bf16[1,512,128]{2,1,0:T(8,128)(2,1)}, u32[]{:S(2)}) copy-start(bf16[1,512,128]{2,1,0:T(8,128)(2,1)} %param.14) | copy-start | bytes 393220
  18.0 105.0 %all-to-all-start = ((bf16[256,8,1024]{2,0,1:T(8,128)(2,1)}), bf16[256,8,1024]{2,0,1:T(8,128)(2,1)}, u32[]{:S(2)}, u32[]{:S(2)}) async-start(bf16[256,8,1024]{2,0,1:T(8,128)(2,1)} %copy.60), calls=%async_computation | async-start | bytes 8388608 | tf_op jit(solution)/shard_map/all_to_all | solution.py:11
  26.6 147.7 %all-gather.4.cloned.1.call-start = ((), (), s32[]{:S(2)}) async-start(), calls=%async_computation.5 | async-start | bytes 1179648 | tf_op jit(solution)/shard_map/all_gather | solution.py:16
  129.4 8.3 %copy-start.5 = (bf16[1,512,256]{2,1,0:T(8,128)(2,1)S(1)}, bf16[1,512,256]{2,1,0:T(8,128)(2,1)}, u32[]{:S(2)}) copy-start(bf16[1,512,256]{2,1,0:T(8,128)(2,1)} %param.12) | copy-start | bytes 786436
  129.4 8.5 %copy-start.1 = (bf16[1,512,128]{2,1,0:T(8,128)(2,1)S(1)}, bf16[1,512,128]{2,1,0:T(8,128)(2,1)}, u32[]{:S(2)}) copy-start(bf16[1,512,128]{2,1,0:T(8,128)(2,1)} %param.13) | copy-start | bytes 393220
  129.4 8.8 %copy-start.3 = (f32[1,1,2,128,128]{4,3,2,1,0:T(8,128)S(1)}, f32[1,1,2,128,128]{4,3,2,1,0:T(8,128)}, u32[]{:S(2)}) copy-start(f32[1,1,2,128,128]{4,3,2,1,0:T(8,128)} %param.17) | copy-start | bytes 393220
  137.6 117.5 %reduce-scatter.3.cloned.1.call-start = ((), (), s32[]{:S(2)}) async-start(), calls=%async_computation.3 | async-start | bytes 8650752 | tf_op jit(solution)/shard_map/reduce_scatter | solution.py:135
  138.3 31.1 %copy-start.4 = (f32[512,512]{1,0:T(8,128)}, f32[512,512]{1,0:T(8,128)S(1)}, u32[]{:S(2)}) copy-start(f32[512,512]{1,0:T(8,128)S(1)} %fusion.55) | copy-start | bytes 3145732
  149.7 138.4 %reduce-scatter.5.cloned.1.call-start = ((), (), s32[]{:S(2)}) async-start(), calls=%async_computation.4 | async-start | bytes 294912 | tf_op jit(solution)/shard_map/reduce_scatter | solution.py:136
  174.3 5.1 %copy-start.6 = (f32[512,1,128]{2,1,0:T(1,128)S(1)}, f32[512,1,128]{2,1,0:T(1,128)}, u32[]{:S(2)}) copy-start(f32[512,1,128]{2,1,0:T(1,128)} %fusion.45) | copy-start | bytes 786436
Sparse Core Ops, SparseCore 0:
  137.8 34.8 all-gather.3
  255.3 32.6 reduce-scatter.4
Sparse Core Ops, SparseCore 1:
  149.7 96.3 reduce-scatter.2
